TPU v7x, 32 devices: a whole 2x2x4 slice. The times are simulated.
32 devices in a mesh: sp: 8 (over z, y), tp: 4 (over x, core).
Axes of the slice: x: 2, y: 2, z: 4, core: 2. Of those that a mesh axis runs over, the one named last changes fastest.
Arguments:
- patches: float32 [160, 240, 256], P('sp', None, 'tp'), may hold values from -6 to 6
- merge_gain: float32 [4, 256], P(None, 'tp'), may hold values from 0.25 to 1.75
- merge_shift: float32 [4, 256], P(None, 'tp'), may hold values from -1.75 to 1.75
- merge_weight: float32 [4, 256, 512], P(None, 'tp'), may hold values from -0.1875 to 0.1875
- first_gain: float32 [2, 512], replicated, may hold values from 0.25 to 1.75
- first_shift: float32 [2, 512], replicated, may hold values from -1.75 to 1.75
- input_weight: float32 [2, 512, 3, 512], P(None, None, None, 'tp'), may hold values from -0.375 to 0.375
- input_bias: float32 [2, 2, 512], P(None, None, 'tp'), may hold values from -1.75 to 1.75
- position_table: float32 [2, 361, 16], P(None, None, 'tp'), may hold values from -6 to 6
- output_weight: float32 [2, 512, 512], P(None, 'tp'), may hold values from -0.75 to 0.75
- output_bias: float32 [2, 512], replicated, may hold values from -1.75 to 1.75
- second_gain: float32 [2, 512], replicated, may hold values from 0.25 to 1.75
- second_shift: float32 [2, 512], replicated, may hold values from -1.75 to 1.75
- expand_weight: float32 [2, 512, 2048], P(None, None, 'tp'), may hold values from -0.25 to 0.25
- expand_bias: float32 [2, 2048], P(None, 'tp'), may hold values from -1.75 to 1.75
- shrink_weight: float32 [2, 2048, 512], P(None, 'tp'), may hold values from -0.1875 to 0.1875
- shrink_bias: float32 [2, 512], replicated, may hold values from -1.75 to 1.75
- page_map: int32 [8, 12], replicated, may hold values from 0 to 58, as said below
- valid_flags: int32 [80, 120], P('sp'), may hold values from 0 to 1, as said below
- cotangent: float32 [80, 120, 512], P('sp', None, 'tp'), may hold values from -6 to 6
Outputs:
- output: float32 [80, 120, 512], P('sp', None, 'tp')
- patches_grad: float32 [160, 240, 256], P('sp', None, 'tp')
- merge_gain_grad: float32 [4, 256], P(None, 'tp')
- merge_shift_grad: float32 [4, 256], P(None, 'tp')
- merge_weight_grad: float32 [4, 256, 512], P(None, 'tp')
- first_gain_grad: float32 [2, 512], replicated
- first_shift_grad: float32 [2, 512], replicated
- input_weight_grad: float32 [2, 512, 3, 512], P(None, None, None, 'tp')
- input_bias_grad: float32 [2, 2, 512], P(None, None, 'tp')
- position_table_grad: float32 [2, 361, 16], P(None, None, 'tp')
- output_weight_grad: float32 [2, 512, 512], P(None, 'tp')
- output_bias_grad: float32 [2, 512], replicated
- second_gain_grad: float32 [2, 512], replicated
- second_shift_grad: float32 [2, 512], replicated
- expand_weight_grad: float32 [2, 512, 2048], P(None, None, 'tp')
- expand_bias_grad: float32 [2, 2048], P(None, 'tp')
- shrink_weight_grad: float32 [2, 2048, 512], P(None, 'tp')
- shrink_bias_grad: float32 [2, 512], replicated
- rms: float32 [5], replicated
Inputs may be any that keep to these rules, and one draw needn't show every extreme that they name: `page_map`: the windows of one page form a rectangle of whole windows; pages are numbered row_page * 13 + column_page, both never falling along their axis, starting at 0 in the first window, with exactly 4 row breaks and 6 column breaks, so the last window holds the largest number. `valid_flags`: the first patch of every window is valid.
All inputs are finite; a program needn't handle non-finite values.
Results may differ from a plain program's by a relative error of at most 0.0003.
Values sent between devices are 32-bit elements; how exact they have to be, the bound alone decides.
A program may use at most 192 MiB of HBM per device.

v0:
```python
import jax
import jax.numpy as jnp
from jax import lax
from jax.sharding import PartitionSpec as P

C = 512
HD = 32
C2 = 256
WIN = 10
SHIFT = 5
highest = lax.Precision.HIGHEST
epsilon = 1e-05
masked = -1000000000.0


def passed_along(block, axis, distance):
    devices = range(lax.axis_size(axis))
    route = [((i - distance) % len(devices), i) for i in devices]
    return lax.ppermute(block, axis, route)


def layer_norm(values, gain_row, offset):
    center = values - jnp.mean(values, axis=-1, keepdims=True)
    spread = jnp.mean(center * center, axis=-1, keepdims=True)
    return center * lax.rsqrt(spread + epsilon) * gain_row + offset


def exact_gelu(values):
    return jax.nn.gelu(values, approximate=False)


def relative_index():
    positions = jnp.arange(WIN * WIN, dtype=jnp.int32)
    row_of = positions // WIN
    column_of = positions % WIN
    row_offset = row_of[:, None] - row_of[None, :] + (WIN - 1)
    column_offset = column_of[:, None] - column_of[None, :] + (WIN - 1)
    return row_offset * (2 * WIN - 1) + column_offset


def window_attention(queries, key_rows, value_rows, bias_grid, region, validity):
    scores = (
        jnp.einsum("wqhd,wkhd->whqk", queries, key_rows, precision=highest) * HD ** (-0.5)
        + bias_grid[None]
    )
    same_region = region[:, :, None] == region[:, None, :]
    diagonal = jnp.eye(WIN * WIN, dtype=bool)[None]
    allowed = same_region & (validity[:, None, :] > 0) | diagonal
    scores = jnp.where(allowed[:, None], scores, masked)
    row_max = jnp.max(scores, axis=-1, keepdims=True)
    weights = jnp.exp(scores - row_max)
    weights = weights / jnp.sum(weights, axis=-1, keepdims=True)
    return jnp.einsum("whqk,wkhd->wqhd", weights, value_rows, precision=highest)


def to_windows(values):
    row_count, column_count = (values.shape[0], values.shape[1])
    trailing = values.shape[2:]
    windowed = values.reshape((row_count // WIN, WIN, column_count // WIN, WIN) + trailing)
    windowed = jnp.moveaxis(windowed, 2, 1)
    return windowed.reshape((row_count // WIN, column_count // WIN, WIN * WIN) + trailing)


def from_windows(windowed, row_count, column_count):
    trailing = windowed.shape[3:]
    values = windowed.reshape((row_count // WIN, column_count // WIN, WIN, WIN) + trailing)
    values = jnp.moveaxis(values, 1, 2)
    return values.reshape((row_count, column_count) + trailing)


def local_attention(window_grid, key_valid, region, table_here, bias_index):
    row_count, column_count = key_valid.shape
    window_count = row_count // WIN * (column_count // WIN)
    local_heads = table_here.shape[1]
    windowed = to_windows(window_grid).reshape(window_count, WIN * WIN, 3, local_heads, HD)
    bias_grid = jnp.transpose(table_here[bias_index], (2, 0, 1))
    attended = window_attention(
        windowed[:, :, 0],
        windowed[:, :, 1],
        windowed[:, :, 2],
        bias_grid,
        to_windows(region).reshape(window_count, WIN * WIN),
        to_windows(key_valid).reshape(window_count, WIN * WIN),
    )
    attended = attended.reshape(row_count // WIN, column_count // WIN, WIN * WIN, local_heads * HD)
    return from_windows(attended, row_count, column_count)


def shifted_region(page_map, sp_index, row_count, column_count, sp_count):
    total_rows = row_count * sp_count
    local_rows = jnp.arange(row_count, dtype=jnp.int32)[:, None]
    root_row = (sp_index * row_count + local_rows + SHIFT) % total_rows
    root_column = (jnp.arange(column_count, dtype=jnp.int32)[None, :] + SHIFT) % column_count
    flat_index = root_row // WIN * page_map.shape[1] + root_column // WIN
    page = jnp.take(page_map.reshape(-1), flat_index)
    wrap_row = (root_row < SHIFT).astype(jnp.int32)
    wrap_column = (root_column < SHIFT).astype(jnp.int32)
    return page * 4 + wrap_row * 2 + wrap_column


def branch_total(partial_value):
    return lax.psum(partial_value, "tp")


def input_total(partial_value):
    return lax.psum(partial_value, "tp")


def shards(
    patches,
    merge_gain,
    merge_shift,
    merge_weight,
    first_gain,
    first_shift,
    input_weight,
    input_bias,
    position_table,
    output_weight,
    output_bias,
    second_gain,
    second_shift,
    expand_weight,
    expand_bias,
    shrink_weight,
    shrink_bias,
    page_map,
    valid_flags,
    cotangent,
):
    row_count, column_count = valid_flags.shape
    tokens = row_count * column_count
    tp_index = lax.axis_index("tp")
    sp_index = lax.axis_index("sp")
    local_width = output_weight.shape[1]
    valid_float = valid_flags.astype(jnp.float32)
    valid_column = valid_float.reshape(tokens, 1)
    bias_index = relative_index()
    region_flat = jnp.zeros((row_count, column_count), jnp.int32)
    region_moved = shifted_region(page_map, sp_index, row_count, column_count, lax.axis_size("sp"))
    full_channels = 4 * C2
    quads = (
        patches.reshape(row_count, 2, column_count, 2, -1)
        .transpose(0, 2, 3, 1, 4)
        .reshape(tokens, 4, -1)
    )
    moments = lax.psum((jnp.sum(quads, axis=(1, 2)), jnp.sum(quads * quads, axis=(1, 2))), "tp")
    center_mean = moments[0] / full_channels
    inverse = lax.rsqrt(moments[1] / full_channels - center_mean * center_mean + epsilon)
    centered = (quads - center_mean[:, None, None]) * inverse[:, None, None]
    merged = centered * merge_gain + merge_shift
    field = branch_total(jnp.einsum("tkc,kcd->td", merged, merge_weight, precision=highest))
    stored = []
    square_list = []
    for block_index in range(2):
        shifted_block = block_index == 1
        normed = layer_norm(field, first_gain[block_index], first_shift[block_index])
        projected = jnp.einsum("td,dkf->tkf", normed, input_weight[block_index], precision=highest)
        bias_rows = jnp.stack(
            [
                input_bias[block_index, 0],
                jnp.zeros_like(input_bias[block_index, 0]),
                input_bias[block_index, 1],
            ]
        )
        window_grid = (projected + bias_rows).reshape(row_count, column_count, 3 * local_width)
        if shifted_block:
            top_rows = passed_along((window_grid[:SHIFT], valid_float[:SHIFT]), "sp", -1)
            window_grid = jnp.roll(
                jnp.concatenate([window_grid[SHIFT:], top_rows[0]], 0), -SHIFT, axis=1
            )
            key_valid = jnp.roll(
                jnp.concatenate([valid_float[SHIFT:], top_rows[1]], 0), -SHIFT, axis=1
            )
            region = region_moved
        else:
            key_valid = valid_float
            region = region_flat
        attended = local_attention(
            window_grid, key_valid, region, position_table[block_index], bias_index
        )
        if shifted_block:
            turned = jnp.roll(attended, SHIFT, axis=1)
            carried = passed_along(turned[row_count - SHIFT :], "sp", 1)
            attended = jnp.concatenate([carried, turned[: row_count - SHIFT]], 0)
        attended = attended.reshape(tokens, local_width)
        mixed_out = (
            branch_total(jnp.dot(attended, output_weight[block_index], precision=highest))
            + output_bias[block_index]
        )
        middle = field + mixed_out
        normed_two = layer_norm(middle, second_gain[block_index], second_shift[block_index])
        pre_act = (
            jnp.dot(normed_two, expand_weight[block_index], precision=highest)
            + expand_bias[block_index]
        )
        hidden = exact_gelu(pre_act)
        branch = (
            branch_total(jnp.dot(hidden, shrink_weight[block_index], precision=highest))
            + shrink_bias[block_index]
        )
        stored.append(
            (
                field,
                normed,
                window_grid,
                key_valid,
                region,
                attended,
                middle,
                normed_two,
                pre_act,
                hidden,
            )
        )
        square_list.append(jnp.sum(mixed_out * mixed_out * valid_column))
        square_list.append(jnp.sum(branch * branch * valid_column))
        field = middle + branch
    square_list.append(jnp.sum(field * field * valid_column))
    square_sums = jnp.stack(square_list)
    valid_count = jnp.sum(valid_float)
    output = lax.dynamic_slice_in_dim(
        field.reshape(row_count, column_count, C), tp_index * local_width, local_width, 2
    )

    def block_backward(block_index, grad_field):
        (
            field_in,
            normed,
            window_grid,
            key_valid,
            region,
            attended,
            middle,
            normed_two,
            pre_act,
            hidden,
        ) = stored[block_index]
        shrink_bias_g = jnp.sum(grad_field, axis=0)
        shrink_weight_g = jnp.dot(hidden.T, grad_field, precision=highest)
        grad_hidden = jnp.dot(grad_field, shrink_weight[block_index].T, precision=highest)
        grad_pre = jax.vjp(exact_gelu, pre_act)[1](grad_hidden)[0]
        expand_bias_g = jnp.sum(grad_pre, axis=0)
        expand_weight_g = jnp.dot(normed_two.T, grad_pre, precision=highest)
        grad_normed_two = input_total(
            jnp.dot(grad_pre, expand_weight[block_index].T, precision=highest)
        )
        pull_second = jax.vjp(
            layer_norm, middle, second_gain[block_index], second_shift[block_index]
        )[1]
        grad_inner, second_gain_g, second_shift_g = pull_second(grad_normed_two)
        grad_middle = grad_field + grad_inner
        output_bias_g = jnp.sum(grad_middle, axis=0)
        output_weight_g = jnp.dot(attended.T, grad_middle, precision=highest)
        grad_attended = jnp.dot(
            grad_middle, output_weight[block_index].T, precision=highest
        ).reshape(row_count, column_count, local_width)
        if block_index == 1:
            upper_rows = passed_along(grad_attended[:SHIFT], "sp", -1)
            grad_attended = jnp.roll(
                jnp.concatenate([grad_attended[SHIFT:], upper_rows], 0), -SHIFT, axis=1
            )

        def attend(grid_in, table_in):
            return local_attention(grid_in, key_valid, region, table_in, bias_index)

        pull_attention = jax.vjp(attend, window_grid, position_table[block_index])[1]
        grad_grid, table_g = pull_attention(grad_attended)
        if block_index == 1:
            turned = jnp.roll(grad_grid, SHIFT, axis=1)
            lower_rows = passed_along(turned[row_count - SHIFT :], "sp", 1)
            grad_grid = jnp.concatenate([lower_rows, turned[: row_count - SHIFT]], 0)
        grad_projected = grad_grid.reshape(tokens, 3, local_width)
        input_bias_g = jnp.stack(
            [jnp.sum(grad_projected[:, 0], axis=0), jnp.sum(grad_projected[:, 2], axis=0)]
        )
        input_weight_g = jnp.einsum("td,tkf->dkf", normed, grad_projected, precision=highest)
        grad_normed = input_total(
            jnp.einsum("tkf,dkf->td", grad_projected, input_weight[block_index], precision=highest)
        )
        pull_first = jax.vjp(
            layer_norm, field_in, first_gain[block_index], first_shift[block_index]
        )[1]
        grad_outer, first_gain_g, first_shift_g = pull_first(grad_normed)
        grads_here = (
            first_gain_g,
            first_shift_g,
            input_weight_g,
            input_bias_g,
            table_g,
            output_weight_g,
            output_bias_g,
            second_gain_g,
            second_shift_g,
            expand_weight_g,
            expand_bias_g,
            shrink_weight_g,
            shrink_bias_g,
        )
        return (grad_middle + grad_outer, grads_here)

    grad_field = lax.all_gather(cotangent, "tp", axis=2, tiled=True).reshape(tokens, C)
    grad_field, late_grads = block_backward(1, grad_field)
    grad_field, early_grads = block_backward(0, grad_field)
    merge_weight_g = jnp.einsum("tkc,td->kcd", merged, grad_field, precision=highest)
    grad_merged = jnp.einsum("td,kcd->tkc", grad_field, merge_weight, precision=highest)
    merge_gain_g = jnp.sum(grad_merged * centered, axis=0)
    merge_shift_g = jnp.sum(grad_merged, axis=0)
    grad_hat = grad_merged * merge_gain
    back_moments = lax.psum(
        (jnp.sum(grad_hat, axis=(1, 2)), jnp.sum(grad_hat * centered, axis=(1, 2))), "tp"
    )
    grad_quads = inverse[:, None, None] * (
        grad_hat
        - back_moments[0][:, None, None] / full_channels
        - centered * back_moments[1][:, None, None] / full_channels
    )
    patches_grad = (
        grad_quads.reshape(row_count, column_count, 2, 2, -1)
        .transpose(0, 3, 1, 2, 4)
        .reshape(2 * row_count, 2 * column_count, -1)
    )
    whole_total = lax.psum(
        (
            early_grads[0],
            early_grads[1],
            early_grads[2],
            early_grads[3],
            early_grads[4],
            early_grads[5],
            early_grads[6],
            early_grads[7],
            early_grads[8],
            early_grads[9],
            early_grads[10],
            early_grads[11],
            early_grads[12],
            late_grads[0],
            late_grads[1],
            late_grads[2],
            late_grads[3],
            late_grads[4],
            late_grads[5],
            late_grads[6],
            late_grads[7],
            late_grads[8],
            late_grads[9],
            late_grads[10],
            late_grads[11],
            late_grads[12],
            merge_gain_g,
            merge_shift_g,
            merge_weight_g,
            square_sums,
            valid_count,
        ),
        "sp",
    )
    early_grads = whole_total[:13]
    late_grads = whole_total[13:26]
    merge_gain_g = whole_total[26]
    merge_shift_g = whole_total[27]
    merge_weight_g = whole_total[28]
    square_sums = whole_total[29]
    valid_count = whole_total[30]
    stacked = [jnp.stack([early_grads[position], late_grads[position]]) for position in range(13)]
    rms = jnp.sqrt(square_sums / (valid_count * C))
    return (
        output,
        patches_grad,
        merge_gain_g,
        merge_shift_g,
        merge_weight_g,
        stacked[0],
        stacked[1],
        stacked[2],
        stacked[3],
        stacked[4],
        stacked[5],
        stacked[6],
        stacked[7],
        stacked[8],
        stacked[9],
        stacked[10],
        stacked[11],
        stacked[12],
        rms,
    )


def solution(mesh):
    placed = (
        P("sp", None, "tp"),
        P(None, "tp"),
        P(None, "tp"),
        P(None, "tp", None),
        P(),
        P(),
        P(None, None, None, "tp"),
        P(None, None, "tp"),
        P(None, None, "tp"),
        P(None, "tp", None),
        P(),
        P(),
        P(),
        P(None, None, "tp"),
        P(None, "tp"),
        P(None, "tp", None),
        P(),
        P(),
        P("sp", None),
        P("sp", None, "tp"),
    )
    return jax.shard_map(
        shards,
        mesh=mesh,
        in_specs=placed,
        out_specs=(
            P("sp", None, "tp"),
            P("sp", None, "tp"),
            P(None, "tp"),
            P(None, "tp"),
            P(None, "tp", None),
            P(),
            P(),
            P(None, None, None, "tp"),
            P(None, None, "tp"),
            P(None, None, "tp"),
            P(None, "tp", None),
            P(),
            P(),
            P(),
            P(None, None, "tp"),
            P(None, "tp"),
            P(None, "tp", None),
            P(),
            P(),
        ),
        check_vma=False,
    )
```

profile of v0, /device:TPU:0, one launch (start us, length us, event | category | flops | bytes accessed | tf_op | source)
XLA Modules:
  0.0 1262.3 jit_solution(3288617347281952883)
XLA Ops:
  8.6 6.0 collective-permute-start.1
  16.5 6.9 fusion.220
  29.1 10.6 all-reduce.9
  47.4 7.3 gather_fusion.1
  56.2 19.6 %gather_fusion = f32[10000,4]{1,0:T(8,128)} fusion(f32[361,4]{1,0:T(8,128)S(1)} %bitcast.327, s32[10240]{0:T(1024)S(1)} %pad_clamp_fusion), kind=kCustom, calls=%fused_computation | custom fusion | bytes 360000 | tf_op jit(solution)/shard_map/gather | solution.py:76
  82.7 16.0 %all-reduce.21.cloned.1.call-done = f32[1200,512]{1,0:T(8,128)} async-done(((f32[1200,512]{1,0:T(8,128)}), f32[1200,512]{1,0:T(8,128)}) %all-reduce.21.cloned.1.call-update) | async-done | bytes 2457616 | tf_op jit(solution)/shard_map/psum | solution.py:102
  102.2 4.3 convolution_add_fusion.3
  106.6 5.5 copy.110
  117.2 6.9 reshape_reshape.21
  124.1 7.1 fusion.234
  138.7 5.9 fusion.246
  161.8 54.7 %all-reduce.23.cloned.1.call-done = f32[1200,512]{1,0:T(8,128)} async-done(((f32[1200,512]{1,0:T(8,128)}), f32[1200,512]{1,0:T(8,128)}) %all-reduce.23.cloned.1.call-update) | async-done | bytes 2457616 | tf_op jit(solution)/shard_map/psum | solution.py:102
  220.8 9.4 fusion
  232.6 5.8 fusion.120
  239.7 56.2 %all-reduce.25.cloned.1.call-done = f32[1200,512]{1,0:T(8,128)} async-done(((f32[1200,512]{1,0:T(8,128)}), f32[1200,512]{1,0:T(8,128)}) %all-reduce.25.cloned.1.call-update) | async-done | bytes 2457616 | tf_op jit(solution)/shard_map/psum | solution.py:102
  300.3 4.4 convolution_add_fusion.2
  309.5 4.2 collective-permute-start
  313.9 19.6 %gather_fusion.2 = f32[10000,4]{1,0:T(8,128)} fusion(f32[361,4]{1,0:T(8,128)S(1)} %bitcast.326, s32[10240]{0:T(1024)S(1)} %pad_clamp_fusion), kind=kCustom, calls=%fused_computation.2 | custom fusion | bytes 360000 | tf_op jit(solution)/shard_map/gather | solution.py:76
  353.2 6.8 reshape_reshape.24
  360.0 6.3 fusion.233
  375.3 5.9 fusion.247
  398.7 11.3 collective-permute-done.2
  416.4 53.2 %all-reduce.27.cloned.1.call-done = f32[1200,512]{1,0:T(8,128)} async-done(((f32[1200,512]{1,0:T(8,128)}), f32[1200,512]{1,0:T(8,128)}) %all-reduce.27.cloned.1.call-update) | async-done | bytes 2457616 | tf_op jit(solution)/shard_map/psum | solution.py:102
  474.8 11.0 fusion.1
  485.9 10.1 all-gather.2.cloned.1.call-done
  496.0 9.2 fusion.248
  506.7 5.6 fusion.115
  512.6 57.1 %all-reduce.29.cloned.1.call-done = f32[1200,512]{1,0:T(8,128)} async-done(((f32[1200,512]{1,0:T(8,128)}), f32[1200,512]{1,0:T(8,128)}) %all-reduce.29.cloned.1.call-update) | async-done | bytes 2457616 | tf_op jit(solution)/shard_map/psum | solution.py:106
  578.7 4.3 collective-permute-start.3
  583.6 5.8 collective-permute-done.3
  601.3 6.2 convolution_bitcast_fusion.7
  607.5 5.1 convert_reduce_fusion.1
  617.2 4.6 fusion.61
  623.6 7.1 copy.141
  630.6 7.3 reshape.689
  648.1 24.0 %collective-permute-done.4 = f32[5,120,384]{2,1,0:T(8,128)S(1)} collective-permute-done((f32[5,120,384]{2,1,0:T(8,128)S(1)}, f32[5,120,384]{2,1,0:T(8,128)S(1)}, u32[]{:S(2)}, u32[]{:S(2)}) %collective-permute-start.4) | collective-permute-done | bytes 921632 | tf_op jit(solution)/shard_map/ppermute | solution.py:19
  677.5 7.4 convolution_bitcast_fusion.2
  685.2 55.1 %all-reduce.31.cloned.1.call-done = f32[1200,512]{1,0:T(8,128)} async-done(((f32[1200,512]{1,0:T(8,128)}), f32[1200,512]{1,0:T(8,128)}) %all-reduce.31.cloned.1.call-update) | async-done | bytes 2457616 | tf_op jit(solution)/shard_map/psum | solution.py:106
  750.0 5.6 fusion.249
  757.1 5.5 fusion.124
  763.7 8.3 fusion.111
  772.0 48.1 %all-reduce.33.cloned.1.call-done = f32[1200,512]{1,0:T(8,128)} async-done(((f32[1200,512]{1,0:T(8,128)}), f32[1200,512]{1,0:T(8,128)}) %all-reduce.33.cloned.1.call-update) | async-done | bytes 2457616 | tf_op jit(solution)/shard_map/psum | solution.py:106
  831.8 5.4 convolution_bitcast_fusion.5
  844.6 6.2 convolution_bitcast_fusion.6
  850.9 5.1 convert_reduce_fusion
  860.6 4.6 fusion.67
  866.9 7.1 copy.150
  874.0 7.3 reshape.694
  885.2 4.3 reshape.695
  889.4 7.4 convolution_bitcast_fusion.1
  897.6 8.4 fusion.49
  906.0 7.4 convolution_bitcast_fusion.3
  915.9 6.0 fusion.56
  921.9 5.9 fusion.50
  927.9 5.8 convolution_bitcast_fusion.4
  936.1 5.8 fusion.51
  942.0 52.5 %all-reduce.37.cloned.1.call-done = (f32[1200,512]{1,0:T(8,128)}, f32[1200,512]{1,0:T(8,128)}) async-done(((f32[1200,512]{1,0:T(8,128)}, f32[1200,512]{1,0:T(8,128)}), (f32[1200,512]{1,0:T(8,128)}, f32[1200,512]{1,0:T(8,128)})) %all-reduce.37.cloned.1.call-update) | async-done | bytes 4915216 | tf_op jit(solution)/shard_map/psum | solution.py:102
  1016.9 56.0 %scatter_custom_fusion.1 = f32[361,4]{1,0:T(8,128)} fusion(s32[10000]{0:T(1024)} %copy-done.91, f32[10000,4]{1,0:T(8,128)} %copy.159, f32[]{:T(128)} %constant.64.clone.1), kind=kCustom, calls=%fused_computation.286 | custom fusion | flops 40000 | bytes 6288 | tf_op jit(solution)/shard_map/transpose(jvp())/scatter-add | solution.py:76
  1082.9 55.5 %scatter_custom_fusion = f32[361,4]{1,0:T(8,128)S(1)} fusion(s32[10000]{0:T(1024)} %copy-done.91, f32[10000,4]{1,0:T(8,128)} %copy.157, f32[]{:T(128)} %constant.64.clone.1), kind=kCustom, calls=%fused_computation.288 | custom fusion | flops 40000 | bytes 6288 | tf_op jit(solution)/shard_map/transpose(jvp())/scatter-add | solution.py:76
  1142.2 7.0 multiply_reduce_fusion.2
  1152.7 6.0 multiply_reduce_fusion.20
  1158.8 51.2 %all-reduce.6 = (f32[4,64]{1,0:T(4,128)}, f32[4,64]{1,0:T(4,128)}, f32[1,512]{1,0:T(1,128)S(1)}, f32[1,512]{1,0:T(1,128)S(1)}, f32[1,512]{1,0:T(1,128)S(1)}, /*i...) all-reduce(f32[4,64]{1,0:T(4,128)S(1)} %get-tuple-element.65, ...), channel_id=1, replica_groups=mesh['sp'=8,'tp'=4] {'sp'}, use_global_device_ids=true, to_apply=%region_44.45 | all-reduce | flops 11086 | bytes 88688 | tf_op jit(solution)/shard_map/psum | solution.py:323
  1210.2 11.0 all-reduce.8
  1240.3 5.8 all-reduce.35.cloned.1.call-done
  (596 shorter events, 291.7 us)
Async XLA Ops:
  7.2 33.1 %copy-start = (f32[4,64,512]{2,1,0:T(8,128)S(1)}, f32[4,64,512]{2,1,0:T(8,128)}, u32[]{:S(2)}) copy-start(f32[4,64,512]{2,1,0:T(8,128)} %param.23) | copy-start | bytes 1572868
  7.2 91.4 %all-reduce.21.cloned.1.call-start = ((), (), s32[]{:S(2)}) async-start(), calls=%async_computation | async-start | bytes 4915200 | tf_op jit(solution)/shard_map/psum | solution.py:102
  8.6 71.9 %collective-permute-start.1 = (f32[5,120]{1,0:T(8,128)S(1)}, f32[5,120]{1,0:T(8,128)S(1)}, u32[]{:S(2)}, u32[]{:S(2)}) collective-permute-start(f32[5,120]{1,0:T(8,128)S(1)} %get-tuple-element.167), channel_id=1, source_target_pairs={{4,0},{8,4},{12,8},{16,12},{20,16},{24,20},{28,24},{0,28},{5,1},{9... | collective-permute-start | bytes 7208 | tf_op jit(solution)/shard_map/ppermute | solution.py:19
  26.8 13.5 %copy-start.117 = (f32[4,64]{1,0:T(4,128)S(1)}, f32[4,64]{1,0:T(4,128)}, u32[]{:S(2)}) copy-start(f32[4,64]{1,0:T(4,128)} %param.21) | copy-start | bytes 3076
  26.8 13.5 %copy-start.173 = (f32[4,64]{1,0:T(4,128)S(1)}, f32[4,64]{1,0:T(4,128)}, u32[]{:S(2)}) copy-start(f32[4,64]{1,0:T(4,128)} %param.22) | copy-start | bytes 3076
  28.9 15.5 %copy-start.18 = (f32[1200,4,64]{0,2,1:T(8,128)}, f32[1200,4,64]{0,2,1:T(8,128)S(1)}, u32[]{:S(2)}) copy-start(f32[1200,4,64]{0,2,1:T(8,128)S(1)} %reshape.680) | copy-start | bytes 3686404
  44.4 172.0 %all-reduce.23.cloned.1.call-start = ((), (), s32[]{:S(2)}) async-start(), calls=%async_computation.1 | async-start | bytes 4915200 | tf_op jit(solution)/shard_map/psum | solution.py:102
  45.8 55.8 %copy-start.133 = (f32[1,512]{1,0:T(1,128)}, f32[1,512]{1,0:T(1,128)S(1)}, u32[]{:S(2)}) copy-start(f32[1,512]{1,0:T(1,128)S(1)} %get-tuple-element.181) | copy-start | bytes 6148
  46.4 55.2 %copy-start.177 = (f32[1,512]{1,0:T(1,128)}, f32[1,512]{1,0:T(1,128)S(1)}, u32[]{:S(2)}) copy-start(f32[1,512]{1,0:T(1,128)S(1)} %get-tuple-element.183) | copy-start | bytes 6148
  47.3 8.2 copy-start.91
  138.7 7.5 copy-start.72
  158.9 137.0 %all-reduce.25.cloned.1.call-start = ((), (), s32[]{:S(2)}) async-start(), calls=%async_computation.2 | async-start | bytes 4915200 | tf_op jit(solution)/shard_map/psum | solution.py:102
  160.0 59.2 %copy-start.145 = (f32[1,512]{1,0:T(1,128)}, f32[1,512]{1,0:T(1,128)S(1)}, u32[]{:S(2)}) copy-start(f32[1,512]{1,0:T(1,128)S(1)} %get-tuple-element.179) | copy-start | bytes 6148
  160.6 59.2 %copy-start.138 = (f32[1,512]{1,0:T(1,128)}, f32[1,512]{1,0:T(1,128)S(1)}, u32[]{:S(2)}) copy-start(f32[1,512]{1,0:T(1,128)S(1)} %get-tuple-element.173) | copy-start | bytes 6148
  161.2 58.6 %copy-start.181 = (f32[1,512]{1,0:T(1,128)}, f32[1,512]{1,0:T(1,128)S(1)}, u32[]{:S(2)}) copy-start(f32[1,512]{1,0:T(1,128)S(1)} %get-tuple-element.175) | copy-start | bytes 6148
  219.2 11.0 copy-start.94
  219.7 10.5 copy-start.107
  219.8 10.5 copy-start.121
  220.8 11.8 copy-start.44
  238.4 231.1 %all-reduce.27.cloned.1.call-start = ((), (), s32[]{:S(2)}) async-start(), calls=%async_computation.3 | async-start | bytes 4915200 | tf_op jit(solution)/shard_map/psum | solution.py:102
  239.7 58.3 %copy-start.147 = (f32[1,512]{1,0:T(1,128)}, f32[1,512]{1,0:T(1,128)S(1)}, u32[]{:S(2)}) copy-start(f32[1,512]{1,0:T(1,128)S(1)} %get-tuple-element.171) | copy-start | bytes 6148
  298.0 6.7 copy-start.1
  298.1 6.7 copy-start.96
  305.8 8.0 copy-start.130
  309.5 34.0 %collective-permute-start = (f32[5,120,384]{2,1,0:T(8,128)}, f32[5,120,384]{2,1,0:T(8,128)}, u32[]{:S(2)}, u32[]{:S(2)}) collective-permute-start(f32[5,120,384]{2,1,0:T(8,128)} %slice.241), channel_id=1, source_target_pairs={{4,0},{8,4},{12,8},{16,12},{20,16},{24,20},{28,24},{0,28},{5,1},{9... | collective-permute-start | bytes 2764808 | tf_op jit(solution)/shard_map/ppermute | solution.py:19
  375.3 7.4 copy-start.74
  394.7 17.2 %copy-start.55 = (f32[2,128,512]{2,1,0:T(8,128)S(1)}, f32[2,128,512]{2,1,0:T(8,128)}, u32[]{:S(2)}) copy-start(f32[2,128,512]{2,1,0:T(8,128)} %param.29) | copy-start | bytes 1572868
  398.7 11.4 collective-permute-start.2
  415.6 80.4 %all-gather.2.cloned.1.call-start = ((), (), s32[]{:S(2)}) async-start(), calls=%async_computation.4 | async-start | bytes 3072000 | tf_op jit(solution)/shard_map/all_gather | solution.py:302
  416.2 153.5 %all-reduce.29.cloned.1.call-start = ((), (), s32[]{:S(2)}) async-start(), calls=%async_computation.5 | async-start | bytes 4915200 | tf_op jit(solution)/shard_map/psum | solution.py:106
  496.0 10.7 copy-start.58
  512.3 227.9 %all-reduce.31.cloned.1.call-start = ((), (), s32[]{:S(2)}) async-start(), calls=%async_computation.6 | async-start | bytes 4915200 | tf_op jit(solution)/shard_map/psum | solution.py:106
  576.5 12.9 %copy-start.10 = (f32[1200,512]{1,0:T(8,128)}, f32[1200,512]{1,0:T(8,128)S(1)}, u32[]{:S(2)}) copy-start(f32[1200,512]{1,0:T(8,128)S(1)} %get-tuple-element.127) | copy-start | bytes 7372804
  576.5 6.4 copy-start.85
  578.7 10.7 collective-permute-start.3
  645.1 27.0 %copy-start.32 = (f32[10,120,384]{2,1,0:T(8,128)S(1)}, f32[10,120,384]{2,1,0:T(8,128)}, u32[]{:S(2)}) copy-start(f32[10,120,384]{2,1,0:T(8,128)} %reshape.690) | copy-start | bytes 5529604
  647.4 24.7 %collective-permute-start.4 = (f32[5,120,384]{2,1,0:T(8,128)S(1)}, f32[5,120,384]{2,1,0:T(8,128)S(1)}, u32[]{:S(2)}, u32[]{:S(2)}) collective-permute-start(f32[5,120,384]{2,1,0:T(8,128)S(1)} %fusion.135), channel_id=1, source_target_pairs={{28,0},{0,4},{4,8},{8,12},{12,16},{16,20},{20,24},{24,28},{29,1},{... | collective-permute-start | bytes 2764808 | tf_op jit(solution)/shard_map/ppermute | solution.py:19
  684.9 55.4 %copy-start.97 = (f32[1200]{0:T(1024)S(1)}, f32[1200]{0:T(1024)}, u32[]{:S(2)}) copy-start(f32[1200]{0:T(1024)} %copy-done.96) | copy-start | bytes 14404
  684.9 55.4 %copy-start.125 = (f32[1200]{0:T(1024)S(1)}, f32[1200]{0:T(1024)}, u32[]{:S(2)}) copy-start(f32[1200]{0:T(1024)} %copy-done.124) | copy-start | bytes 14404
  684.9 59.5 %copy-start.110 = (f32[1200]{0:T(1024)S(1)}, f32[1200]{0:T(1024)}, u32[]{:S(2)}) copy-start(f32[1200]{0:T(1024)} %copy-done.109) | copy-start | bytes 14404
  684.9 135.2 %all-reduce.33.cloned.1.call-start = ((), (), s32[]{:S(2)}) async-start(), calls=%async_computation.7 | async-start | bytes 4915200 | tf_op jit(solution)/shard_map/psum | solution.py:106
  747.0 8.6 copy-start.13
  750.0 7.1 copy-start.59
  762.6 231.9 %all-reduce.37.cloned.1.call-start = ((), (), s32[]{:S(2)}) async-start(), calls=%async_computation.9 | async-start | bytes 9830400 | tf_op jit(solution)/shard_map/psum | solution.py:102
  763.7 56.4 %copy-start.95 = (f32[1200]{0:T(1024)S(1)}, f32[1200]{0:T(1024)}, u32[]{:S(2)}) copy-start(f32[1200]{0:T(1024)} %copy-done.94) | copy-start | bytes 14404
  772.0 51.5 %copy-start.108 = (f32[1200]{0:T(1024)S(1)}, f32[1200]{0:T(1024)}, u32[]{:S(2)}) copy-start(f32[1200]{0:T(1024)} %copy-done.107) | copy-start | bytes 14404
  838.3 6.2 copy-start.83
  844.6 6.3 copy-start.21
  844.6 6.3 copy-start.73
  844.6 6.3 copy-start.77
  844.6 6.3 copy-start.131
  896.9 349.2 %all-reduce.35.cloned.1.call-start = ((), (), s32[]{:S(2)}) async-start(), calls=%async_computation.8 | async-start | bytes 13631488 | tf_op jit(solution)/shard_map/psum | solution.py:323
  897.5 8.4 copy-start.17
  897.5 8.4 copy-start.30
  906.0 7.4 copy-start.12
  906.0 7.4 copy-start.49
  906.0 9.8 copy-start.33
  915.9 11.9 copy-start.29
  927.9 8.3 copy-start.34
  1013.5 63.1 %copy-start.104 = (f32[6,8,100]{2,1,0:T(8,128)S(1)}, f32[6,8,100]{2,1,0:T(8,128)}, u32[]{:S(2)}) copy-start(f32[6,8,100]{2,1,0:T(8,128)} %copy-done.103) | copy-start | bytes 57604
  1079.4 62.8 %copy-start.144 = (f32[1,512]{1,0:T(1,128)S(1)}, f32[1,512]{1,0:T(1,128)}, u32[]{:S(2)}) copy-start(f32[1,512]{1,0:T(1,128)} %get-tuple-element.178) | copy-start | bytes 6148
  1079.5 62.7 %copy-start.146 = (f32[1,512]{1,0:T(1,128)S(1)}, f32[1,512]{1,0:T(1,128)}, u32[]{:S(2)}) copy-start(f32[1,512]{1,0:T(1,128)} %copy-done.145) | copy-start | bytes 6148
  1079.5 62.7 %copy-start.148 = (f32[1,512]{1,0:T(1,128)S(1)}, f32[1,512]{1,0:T(1,128)}, u32[]{:S(2)}) copy-start(f32[1,512]{1,0:T(1,128)} %copy-done.147) | copy-start | bytes 6148
  1079.5 62.7 %copy-start.164 = (f32[1,512]{1,0:T(1,128)S(1)}, f32[1,512]{1,0:T(1,128)}, u32[]{:S(2)}) copy-start(f32[1,512]{1,0:T(1,128)} %get-tuple-element.170) | copy-start | bytes 6148
  (137 other events, 485.2 us)
Sparse Core Ops, SparseCore 0:
  44.5 54.0 all-reduce.20
  159.1 57.3 all-reduce.22
  238.6 57.3 all-reduce.24
  415.7 53.8 all-reduce.26
  470.9 25.0 all-gather.1
  512.4 57.2 all-reduce.28
  685.0 55.1 all-reduce.30
  762.7 57.3 all-reduce.32
  897.0 97.4 all-reduce.36
  1005.2 240.7 all-reduce.34
where the time goes:
time: 1270 us; the launch traced here: 1260 us
  waiting for transfers between devices  451 us (36%)
  local copies, waits for them, and re-layouts  279 us (22%)
  matrix products  214 us (17%)
  other arithmetic  211 us (17%)
  blocking collectives  72.8 us (6%)
  starting transfers between devices  17.9 us (1%)
  between operations  17.3 us (1%)
    psum x5, waiting for transfers between devices, branch_total(): return lax.psum(partial_value, 'tp')  233 us
    psum x3, waiting for transfers between devices, input_total(): return lax.psum(partial_value, 'tp')  160 us
    scatter-add x2, other arithmetic, local_attention(): bias_grid = jnp.transpose(table_here[bias_index], (2, 0, 1))  112 us
    psum x1, blocking collectives, shards(): lax.psum((early_grads[0], early_grads[1], early_grads[2], early_grads[3],...  51.2 us
    unnamed x384, local copies, waits for them, and re-layouts  47.3 us
    gather x6, local copies, waits for them, and re-layouts, local_attention(): bias_grid = jnp.transpose(table_here[bias_index], (2, 0, 1))  46.7 us
    ppermute x5, waiting for transfers between devices, passed_along(): return lax.ppermute(block, axis, route)  41.2 us
    dot_general x6, matrix products, window_attention(): return jnp.einsum('whqk,wkhd->wqhd', weights, value_rows, precision=highest)  29.6 us
  transfers between devices with their start and end apart: 15, of which 13 were waited for; matrix products, arithmetic and copies ran while one was open for 26% of the time, Pallas kernels for 0%

commit v1 on v0

--- a/solution.py
+++ b/solution.py
@@ -103,7 +103,7 @@
 
 
 def input_total(partial_value):
-    return lax.psum(partial_value, "tp")
+    return lax.all_gather(partial_value, "tp").sum(axis=0)
 
 
 def shards(

time: 1270 us -> 1360 us (1.071)
  other arithmetic: 211 us -> 257 us
  waiting for transfers between devices: 451 us -> 490 us
    all_gather x0 -> x4, waiting for transfers between devices: none -> 207 us  [input_total(): return lax.all_gather(partial_value, 'tp').sum(axis=0)]
    psum x3 -> x0, waiting for transfers between devices: 160 us -> none  [input_total(): return lax.psum(partial_value, 'tp')]
    reduce_sum x1 -> x4, other arithmetic: 7 us -> 27 us  [input_total(): return lax.all_gather(partial_value, 'tp').sum(axis=0)]
    reduce_sum x4 -> x8, other arithmetic: 15.6 us -> 33.8 us  [layer_norm(): return center * lax.rsqrt(spread + epsilon) * gain_row + offset]
    unnamed x384 -> x348, local copies, waits for them, and re-layouts: 47.3 us -> 47.3 us
  transfers between devices with their start and end apart: 15 -> 16, of which waited for: 13 -> 13; matrix products, arithmetic and copies ran while one was open for 26% -> 26% of each run, Pallas kernels for 0% -> 0%
where the time goes in v1:
time: 1360 us; the launch traced here: 1350 us
  waiting for transfers between devices  490 us (36%)
  local copies, waits for them, and re-layouts  278 us (20%)
  other arithmetic  257 us (19%)
  matrix products  214 us (16%)
  blocking collectives  74.2 us (5%)
  between operations  17.2 us (1%)
  starting transfers between devices  17 us (1%)
    psum x5, waiting for transfers between devices, branch_total(): return lax.psum(partial_value, 'tp')  231 us
    all_gather x4, waiting for transfers between devices, input_total(): return lax.all_gather(partial_value, 'tp').sum(axis=0)  207 us
    scatter-add x2, other arithmetic, local_attention(): bias_grid = jnp.transpose(table_here[bias_index], (2, 0, 1))  112 us
    psum x1, blocking collectives, shards(): lax.psum((early_grads[0], early_grads[1], early_grads[2], early_grads[3],...  52.3 us
    unnamed x348, local copies, waits for them, and re-layouts  47.3 us
    gather x6, local copies, waits for them, and re-layouts, local_attention(): bias_grid = jnp.transpose(table_here[bias_index], (2, 0, 1))  46.4 us
    ppermute x5, waiting for transfers between devices, passed_along(): return lax.ppermute(block, axis, route)  41.2 us
    reduce_sum x8, other arithmetic, layer_norm(): return center * lax.rsqrt(spread + epsilon) * gain_row + offset  33.8 us
  transfers between devices with their start and end apart: 16, of which 13 were waited for; matrix products, arithmetic and copies ran while one was open for 26% of the time, Pallas kernels for 0%

profile of v1, /device:TPU:0, one launch (start us, length us, event | category | flops | bytes accessed | tf_op | source)
XLA Modules:
  0.0 1348.2 jit_solution(1650888553545840373)
XLA Ops:
  8.6 6.0 collective-permute-start.1
  16.5 6.9 fusion.220
  29.1 10.6 all-reduce.9
  45.4 7.3 gather_fusion.1
  53.6 19.5 %gather_fusion = f32[10000,4]{1,0:T(8,128)} fusion(f32[361,4]{1,0:T(8,128)S(1)} %bitcast.331, s32[10240]{0:T(1024)S(1)} %pad_clamp_fusion), kind=kCustom, calls=%fused_computation | custom fusion | bytes 360000 | tf_op jit(solution)/shard_map/gather | solution.py:76
  79.8 18.8 %all-reduce.17.cloned.1.call-done = f32[1200,512]{1,0:T(8,128)} async-done(((f32[1200,512]{1,0:T(8,128)}), f32[1200,512]{1,0:T(8,128)}) %all-reduce.17.cloned.1.call-update) | async-done | bytes 2457616 | tf_op jit(solution)/shard_map/psum | solution.py:102
  106.6 5.5 copy.110
  117.2 7.2 reshape_reshape.21
  124.4 7.1 fusion.234
  138.9 5.9 fusion.246
  161.6 54.9 %all-reduce.19.cloned.1.call-done = f32[1200,512]{1,0:T(8,128)} async-done(((f32[1200,512]{1,0:T(8,128)}), f32[1200,512]{1,0:T(8,128)}) %all-reduce.19.cloned.1.call-update) | async-done | bytes 2457616 | tf_op jit(solution)/shard_map/psum | solution.py:102
  220.9 9.4 fusion
  232.5 6.0 fusion.120
  239.8 56.2 %all-reduce.21.cloned.1.call-done = f32[1200,512]{1,0:T(8,128)} async-done(((f32[1200,512]{1,0:T(8,128)}), f32[1200,512]{1,0:T(8,128)}) %all-reduce.21.cloned.1.call-update) | async-done | bytes 2457616 | tf_op jit(solution)/shard_map/psum | solution.py:102
  314.0 19.5 %gather_fusion.2 = f32[10000,4]{1,0:T(8,128)} fusion(f32[361,4]{1,0:T(8,128)S(1)} %bitcast.330, s32[10240]{0:T(1024)S(1)} %pad_clamp_fusion), kind=kCustom, calls=%fused_computation.2 | custom fusion | bytes 360000 | tf_op jit(solution)/shard_map/gather | solution.py:76
  353.3 6.8 reshape_reshape.24
  360.1 6.4 fusion.233
  375.2 5.9 fusion.247
  398.6 11.3 collective-permute-done.2
  416.4 52.9 %all-reduce.23.cloned.1.call-done = f32[1200,512]{1,0:T(8,128)} async-done(((f32[1200,512]{1,0:T(8,128)}), f32[1200,512]{1,0:T(8,128)}) %all-reduce.23.cloned.1.call-update) | async-done | bytes 2457616 | tf_op jit(solution)/shard_map/psum | solution.py:102
  474.6 11.1 fusion.1
  485.7 10.1 all-gather.10.cloned.1.call-done
  495.8 9.2 fusion.248
  506.5 5.5 fusion.115
  512.2 8.2 fusion.111
  521.9 56.7 %all-gather.12.cloned.1.call-done = f32[4800,512]{1,0:T(8,128)} async-done(((f32[1200,512]{1,0:T(8,128)}), f32[4800,512]{1,0:T(8,128)}) %all-gather.12.cloned.1.call-update) | async-done | bytes 9830416 | tf_op jit(solution)/shard_map/all_gather | solution.py:106
  578.6 6.7 reduce_sum.555
  590.2 48.0 %all-reduce.25.cloned.1.call-done = f32[1200,512]{1,0:T(8,128)} async-done(((f32[1200,512]{1,0:T(8,128)}), f32[1200,512]{1,0:T(8,128)}) %all-reduce.25.cloned.1.call-update) | async-done | bytes 2457616 | tf_op jit(solution)/shard_map/psum | solution.py:102
  638.3 8.8 fusion.229
  655.1 5.8 collective-permute-done.3
  672.5 6.2 convolution_bitcast_fusion.7
  678.8 5.1 convert_reduce_fusion.1
  688.7 4.6 fusion.61
  695.1 7.0 copy.141
  702.1 7.2 reshape.689
  719.6 24.0 %collective-permute-done.4 = f32[5,120,384]{2,1,0:T(8,128)S(1)} collective-permute-done((f32[5,120,384]{2,1,0:T(8,128)S(1)}, f32[5,120,384]{2,1,0:T(8,128)S(1)}, u32[]{:S(2)}, u32[]{:S(2)}) %collective-permute-start.4) | collective-permute-done | bytes 921632 | tf_op jit(solution)/shard_map/ppermute | solution.py:19
  749.0 7.4 convolution_bitcast_fusion.2
  756.6 64.3 %all-gather.14.cloned.1.call-done = f32[4800,512]{1,0:T(8,128)} async-done(((f32[1200,512]{1,0:T(8,128)}), f32[4800,512]{1,0:T(8,128)}) %all-gather.14.cloned.1.call-update) | async-done | bytes 9830416 | tf_op jit(solution)/shard_map/all_gather | solution.py:106
  820.9 6.7 reduce_sum.567
  837.3 5.6 fusion.249
  844.4 5.8 fusion.124
  851.5 65.3 %all-gather.16.cloned.1.call-done = f32[4800,512]{1,0:T(8,128)} async-done(((f32[1200,512]{1,0:T(8,128)}), f32[4800,512]{1,0:T(8,128)}) %all-gather.16.cloned.1.call-update) | async-done | bytes 9830416 | tf_op jit(solution)/shard_map/all_gather | solution.py:106
  916.8 6.7 reduce_sum.573
  935.2 5.4 convolution_bitcast_fusion.5
  948.3 6.2 convolution_bitcast_fusion.6
  954.5 5.2 convert_reduce_fusion
  970.5 7.1 copy.150
  977.6 7.2 reshape.694
  993.0 7.3 convolution_bitcast_fusion.1
  1001.1 8.4 fusion.49
  1009.6 7.7 convolution_bitcast_fusion.3
  1019.8 6.2 fusion.56
  1026.1 5.9 fusion.50
  1032.1 5.7 convolution_bitcast_fusion.4
  1040.3 5.9 fusion.51
  1046.1 20.9 %all-gather.18.cloned.1.call-done = f32[4800,512]{1,0:T(8,128)} async-done(((f32[1200,512]{1,0:T(8,128)}), f32[4800,512]{1,0:T(8,128)}) %all-gather.18.cloned.1.call-update) | async-done | bytes 9830416 | tf_op jit(solution)/shard_map/all_gather | solution.py:106
  1067.1 6.7 reduce_sum.582
  1090.8 5.1 reduce_sum.622
  1105.7 56.2 %scatter_custom_fusion.1 = f32[361,4]{1,0:T(8,128)} fusion(s32[10000]{0:T(1024)} %copy-done.88, f32[10000,4]{1,0:T(8,128)} %copy.159, f32[]{:T(128)} %constant.64.clone.1), kind=kCustom, calls=%fused_computation.286 | custom fusion | flops 40000 | bytes 6288 | tf_op jit(solution)/shard_map/transpose(jvp())/scatter-add | solution.py:76
  1176.3 55.4 %scatter_custom_fusion = f32[361,4]{1,0:T(8,128)S(1)} fusion(s32[10000]{0:T(1024)} %copy-done.88, f32[10000,4]{1,0:T(8,128)} %copy.157, f32[]{:T(128)} %constant.64.clone.1), kind=kCustom, calls=%fused_computation.288 | custom fusion | flops 40000 | bytes 6288 | tf_op jit(solution)/shard_map/transpose(jvp())/scatter-add | solution.py:76
  1231.7 4.8 reduce_sum.618
  1244.8 6.1 multiply_reduce_fusion.20
  1251.0 52.3 %all-reduce.6 = (f32[4,64]{1,0:T(4,128)}, f32[4,64]{1,0:T(4,128)}, f32[1,512]{1,0:T(1,128)S(1)}, f32[1,512]{1,0:T(1,128)S(1)}, f32[1,512]{1,0:T(1,128)S(1)}, /*i...) all-reduce(f32[4,64]{1,0:T(4,128)S(1)} %get-tuple-element.65, ...), channel_id=1, replica_groups=mesh['sp'=8,'tp'=4] {'sp'}, use_global_device_ids=true, to_apply=%region_44.45 | all-reduce | flops 11086 | bytes 88688 | tf_op jit(solution)/shard_map/psum | solution.py:323
  1303.5 11.3 all-reduce.8
  (570 shorter events, 323.2 us)
Async XLA Ops:
  7.2 33.1 %copy-start = (f32[4,64,512]{2,1,0:T(8,128)S(1)}, f32[4,64,512]{2,1,0:T(8,128)}, u32[]{:S(2)}) copy-start(f32[4,64,512]{2,1,0:T(8,128)} %param.23) | copy-start | bytes 1572868
  7.2 91.4 %all-reduce.17.cloned.1.call-start = ((), (), s32[]{:S(2)}) async-start(), calls=%async_computation | async-start | bytes 4915200 | tf_op jit(solution)/shard_map/psum | solution.py:102
  8.6 69.1 %collective-permute-start.1 = (f32[5,120]{1,0:T(8,128)S(1)}, f32[5,120]{1,0:T(8,128)S(1)}, u32[]{:S(2)}, u32[]{:S(2)}) collective-permute-start(f32[5,120]{1,0:T(8,128)S(1)} %get-tuple-element.167), channel_id=1, source_target_pairs={{4,0},{8,4},{12,8},{16,12},{20,16},{24,20},{28,24},{0,28},{5,1},{9... | collective-permute-start | bytes 7208 | tf_op jit(solution)/shard_map/ppermute | solution.py:19
  26.8 13.5 %copy-start.114 = (f32[4,64]{1,0:T(4,128)S(1)}, f32[4,64]{1,0:T(4,128)}, u32[]{:S(2)}) copy-start(f32[4,64]{1,0:T(4,128)} %param.21) | copy-start | bytes 3076
  26.8 13.5 %copy-start.155 = (f32[4,64]{1,0:T(4,128)S(1)}, f32[4,64]{1,0:T(4,128)}, u32[]{:S(2)}) copy-start(f32[4,64]{1,0:T(4,128)} %param.22) | copy-start | bytes 3076
  28.9 15.5 %copy-start.17 = (f32[1200,4,64]{0,2,1:T(8,128)}, f32[1200,4,64]{0,2,1:T(8,128)S(1)}, u32[]{:S(2)}) copy-start(f32[1200,4,64]{0,2,1:T(8,128)S(1)} %reshape.680) | copy-start | bytes 3686404
  44.4 172.1 %all-reduce.19.cloned.1.call-start = ((), (), s32[]{:S(2)}) async-start(), calls=%async_computation.1 | async-start | bytes 4915200 | tf_op jit(solution)/shard_map/psum | solution.py:102
  44.9 56.7 %copy-start.125 = (f32[1,512]{1,0:T(1,128)}, f32[1,512]{1,0:T(1,128)S(1)}, u32[]{:S(2)}) copy-start(f32[1,512]{1,0:T(1,128)S(1)} %get-tuple-element.181) | copy-start | bytes 6148
  44.9 253.7 %copy-start.127 = (f32[1,512]{1,0:T(1,128)}, f32[1,512]{1,0:T(1,128)S(1)}, u32[]{:S(2)}) copy-start(f32[1,512]{1,0:T(1,128)S(1)} %get-tuple-element.180) | copy-start | bytes 6148
  44.9 56.6 %copy-start.159 = (f32[1,512]{1,0:T(1,128)}, f32[1,512]{1,0:T(1,128)S(1)}, u32[]{:S(2)}) copy-start(f32[1,512]{1,0:T(1,128)S(1)} %get-tuple-element.183) | copy-start | bytes 6148
  45.0 253.7 %copy-start.161 = (f32[1,512]{1,0:T(1,128)}, f32[1,512]{1,0:T(1,128)S(1)}, u32[]{:S(2)}) copy-start(f32[1,512]{1,0:T(1,128)S(1)} %get-tuple-element.182) | copy-start | bytes 6148
  45.4 7.6 copy-start.88
  138.9 7.4 copy-start.70
  159.0 137.0 %all-reduce.21.cloned.1.call-start = ((), (), s32[]{:S(2)}) async-start(), calls=%async_computation.2 | async-start | bytes 4915200 | tf_op jit(solution)/shard_map/psum | solution.py:102
  159.8 59.4 %copy-start.135 = (f32[1,512]{1,0:T(1,128)}, f32[1,512]{1,0:T(1,128)S(1)}, u32[]{:S(2)}) copy-start(f32[1,512]{1,0:T(1,128)S(1)} %get-tuple-element.179) | copy-start | bytes 6148
  160.4 59.4 %copy-start.130 = (f32[1,512]{1,0:T(1,128)}, f32[1,512]{1,0:T(1,128)S(1)}, u32[]{:S(2)}) copy-start(f32[1,512]{1,0:T(1,128)S(1)} %get-tuple-element.173) | copy-start | bytes 6148
  161.0 58.8 %copy-start.163 = (f32[1,512]{1,0:T(1,128)}, f32[1,512]{1,0:T(1,128)S(1)}, u32[]{:S(2)}) copy-start(f32[1,512]{1,0:T(1,128)S(1)} %get-tuple-element.175) | copy-start | bytes 6148
  219.3 11.0 copy-start.93
  219.8 10.5 copy-start.105
  219.8 10.5 copy-start.118
  220.9 11.6 copy-start.42
  238.5 230.8 %all-reduce.23.cloned.1.call-start = ((), (), s32[]{:S(2)}) async-start(), calls=%async_computation.3 | async-start | bytes 4915200 | tf_op jit(solution)/shard_map/psum | solution.py:102
  239.8 58.3 %copy-start.136 = (f32[1,512]{1,0:T(1,128)}, f32[1,512]{1,0:T(1,128)S(1)}, u32[]{:S(2)}) copy-start(f32[1,512]{1,0:T(1,128)S(1)} %get-tuple-element.171) | copy-start | bytes 6148
  298.1 6.7 copy-start.1
  298.1 6.7 copy-start.95
  309.6 33.9 %collective-permute-start = (f32[5,120,384]{2,1,0:T(8,128)}, f32[5,120,384]{2,1,0:T(8,128)}, u32[]{:S(2)}, u32[]{:S(2)}) collective-permute-start(f32[5,120,384]{2,1,0:T(8,128)} %slice.241), channel_id=1, source_target_pairs={{4,0},{8,4},{12,8},{16,12},{20,16},{24,20},{28,24},{0,28},{5,1},{9... | collective-permute-start | bytes 2764808 | tf_op jit(solution)/shard_map/ppermute | solution.py:19
  375.2 7.4 copy-start.72
  394.6 17.2 %copy-start.53 = (f32[2,128,512]{2,1,0:T(8,128)S(1)}, f32[2,128,512]{2,1,0:T(8,128)}, u32[]{:S(2)}) copy-start(f32[2,128,512]{2,1,0:T(8,128)} %param.29) | copy-start | bytes 1572868
  398.5 11.4 collective-permute-start.2
  415.3 80.4 %all-gather.10.cloned.1.call-start = ((), (), s32[]{:S(2)}) async-start(), calls=%async_computation.5 | async-start | bytes 3072000 | tf_op jit(solution)/shard_map/all_gather | solution.py:302
  415.9 162.7 %all-gather.12.cloned.1.call-start = ((), (), s32[]{:S(2)}) async-start(), calls=%async_computation.6 | async-start | bytes 12288000 | tf_op jit(solution)/shard_map/all_gather | solution.py:106
  495.8 10.7 copy-start.56
  512.0 126.3 %all-reduce.25.cloned.1.call-start = ((), (), s32[]{:S(2)}) async-start(), calls=%async_computation.4 | async-start | bytes 4915200 | tf_op jit(solution)/shard_map/psum | solution.py:102
  520.4 300.5 %all-gather.14.cloned.1.call-start = ((), (), s32[]{:S(2)}) async-start(), calls=%async_computation.7 | async-start | bytes 12288000 | tf_op jit(solution)/shard_map/all_gather | solution.py:106
  638.3 8.8 copy-start.14
  648.0 12.9 copy-start.8
  650.2 10.7 collective-permute-start.3
  672.5 6.3 copy-start.22
  672.5 6.3 copy-start.73
  672.5 6.3 copy-start.74
  672.5 6.3 copy-start.124
  716.6 27.0 %copy-start.34 = (f32[10,120,384]{2,1,0:T(8,128)S(1)}, f32[10,120,384]{2,1,0:T(8,128)}, u32[]{:S(2)}) copy-start(f32[10,120,384]{2,1,0:T(8,128)} %reshape.690) | copy-start | bytes 5529604
  719.0 24.7 %collective-permute-start.4 = (f32[5,120,384]{2,1,0:T(8,128)S(1)}, f32[5,120,384]{2,1,0:T(8,128)S(1)}, u32[]{:S(2)}, u32[]{:S(2)}) collective-permute-start(f32[5,120,384]{2,1,0:T(8,128)S(1)} %fusion.135), channel_id=1, source_target_pairs={{28,0},{0,4},{4,8},{8,12},{12,16},{16,20},{20,24},{24,28},{29,1},{... | collective-permute-start | bytes 2764808 | tf_op jit(solution)/shard_map/ppermute | solution.py:19
  756.3 160.5 %all-gather.16.cloned.1.call-start = ((), (), s32[]{:S(2)}) async-start(), calls=%async_computation.8 | async-start | bytes 12288000 | tf_op jit(solution)/shard_map/all_gather | solution.py:106
  820.9 6.7 copy-start.96
  820.9 6.7 copy-start.121
  820.9 6.8 copy-start.128
  834.3 8.6 copy-start.11
  837.3 7.0 copy-start.57
  850.2 216.9 %all-gather.18.cloned.1.call-start = ((), (), s32[]{:S(2)}) async-start(), calls=%async_computation.9 | async-start | bytes 12288000 | tf_op jit(solution)/shard_map/all_gather | solution.py:106
  916.8 6.7 copy-start.94
  916.8 6.7 copy-start.119
  941.7 6.5 copy-start.81
  1000.4 331.5 %all-reduce.27.cloned.1.call-start = ((), (), s32[]{:S(2)}) async-start(), calls=%async_computation.10 | async-start | bytes 13631488 | tf_op jit(solution)/shard_map/psum | solution.py:323
  1001.1 8.4 copy-start.15
  1001.1 8.4 copy-start.29
  1009.5 7.8 copy-start.10
  1009.6 7.8 copy-start.47
  1009.6 10.2 copy-start.35
  1019.8 6.3 copy-start.41
  1019.8 12.2 copy-start.28
  1032.0 8.2 copy-start.36
  1090.8 7.0 copy-start.64
  1090.8 7.0 copy-start.98
  (120 other events, 405.8 us)
Sparse Core Ops, SparseCore 0:
  44.5 54.0 all-reduce.16
  159.1 57.3 all-reduce.18
  238.6 57.3 all-reduce.20
  415.5 53.8 all-reduce.22
  470.7 25.0 all-gather.9
  512.1 66.4 all-gather.11
  581.0 57.2 all-reduce.24
  756.5 64.3 all-gather.13
  850.3 66.4 all-gather.15
  1000.5 66.4 all-gather.17
  1084.1 240.5 all-reduce.26
